TPU v7x, 32 devices: a whole 2x2x4 slice. The times are simulated.
32 devices in a mesh: ens: 2 (over y), row: 4 (over z), col: 4 (over x, core).
Axes of the slice: x: 2, y: 2, z: 4, core: 2. Of those that a mesh axis runs over, the one named last changes fastest.
Arguments:
- series: float32 [24576, 256], P(('ens', 'row', 'col')), parts along dimension 0, may hold values from -22 to 22, as said below
- vectors: float32 [24576, 128], P(('ens', 'row', 'col')), parts along dimension 0, may hold values from -6 to 6
- damp_class: int32 [24576], P(('ens', 'row', 'col')), parts along dimension 0, may hold values from 0 to 15
- damp_levels: float32 [16], replicated, may hold values from 0.5 to 2
- removed_blocks: int32 [64, 32], P('ens'), parts along dimension 0, may hold values 0 or 1
Outputs:
- filtered: float32 [24576, 128], P(('ens', 'row', 'col')), parts along dimension 0
There are 2 independent parts, one for each index of `ens`. A program takes and returns all parts, laid end to end along the dimension named above; an argument that names none is the same for every part. Nothing has to cross between parts.
Inputs may be any that keep to these rules, and one draw needn't show every extreme that they name: Each voxel's series is not constant.
All inputs are finite; a program needn't handle non-finite values.
Results may differ from a plain program's by a relative error of at most 0.0003.
Values sent between devices are 32-bit elements; how exact they have to be, the bound alone decides.
No kernel may reach another device: no remote copies, remote signals or barrier semaphores. Data moves between devices by JAX's collectives and lax.ppermute only.
A program may use at most 128 MiB of HBM per device.

v0:
```python
import jax
import jax.numpy as jnp
from jax import lax
from jax.sharding import PartitionSpec as P

N = 12288
sharpness = 12.0


def standardize(series):
    centered = series - jnp.mean(series, axis=1, keepdims=True)
    spread = jnp.mean(centered * centered, axis=1, keepdims=True)
    return centered * lax.rsqrt(spread + 1e-05)


def local(series, vectors, damp_class, damp_levels, removed_blocks):
    n_col = lax.axis_size("col")
    row_id = lax.axis_index("row")
    col_id = lax.axis_index("col")
    shard_rows = series.shape[0]
    samples = series.shape[1]
    classes = damp_levels.shape[0]
    z_own = standardize(series)
    onehot = (damp_class[:, None] == jnp.arange(classes, dtype=jnp.int32)[None, :]).astype(
        jnp.float32
    )
    damping = jnp.sum(onehot * damp_levels[None, :], axis=1)
    z_rows, d_rows = (
        lax.all_gather(z_own, "col", axis=0, tiled=True),
        lax.all_gather(damping, "col", axis=0, tiled=True),
    )
    tile_rows = z_rows.shape[0]
    blocks = removed_blocks.shape[0]
    block_size = N // blocks
    row_blocks = tile_rows // block_size
    keep_rows = 1.0 - lax.dynamic_slice_in_dim(
        removed_blocks, row_id * row_blocks, row_blocks, 0
    ).astype(jnp.float32)
    shard_piece = lax.all_gather(z_own, "row", axis=0, tiled=True)
    count = shard_piece.shape[0]
    position = jnp.arange(count, dtype=jnp.int32)
    owner_row = position // shard_rows
    global_index = (owner_row * n_col + col_id) * shard_rows + position % shard_rows
    col_block = global_index // block_size
    onehot_cols = (col_block[None, :] == jnp.arange(blocks, dtype=jnp.int32)[:, None]).astype(
        jnp.float32
    )
    keep_small = jnp.dot(
        keep_rows, onehot_cols, precision=lax.Precision.HIGHEST, preferred_element_type=jnp.float32
    )
    keep_full = jnp.broadcast_to(keep_small[:, None, :], (row_blocks, block_size, count)).reshape(
        tile_rows, count
    )
    correlation = (
        lax.dot_general(
            z_rows,
            shard_piece,
            (((1,), (1,)), ((), ())),
            precision=lax.Precision.HIGHEST,
            preferred_element_type=jnp.float32,
        )
        / samples
    )
    affinity = jnp.tanh(sharpness * correlation) * keep_full * d_rows[:, None]
    spectral_scale = 0.5 * N * jnp.mean(damp_levels * damp_levels)

    def forward_add(shard_piece):
        return jnp.dot(
            affinity,
            shard_piece,
            precision=lax.Precision.HIGHEST,
            preferred_element_type=jnp.float32,
        )

    def backward_add(shard_piece):
        return lax.dot_general(
            affinity,
            shard_piece,
            (((0,), (0,)), ((), ())),
            precision=lax.Precision.HIGHEST,
            preferred_element_type=jnp.float32,
        )

    def normal_apply(field_in):
        product = forward_add(lax.all_gather(field_in, "row", axis=0, tiled=True))
        product = lax.psum_scatter(product, "col", scatter_dimension=0, tiled=True)
        returned = backward_add(lax.all_gather(product, "col", axis=0, tiled=True))
        return lax.psum_scatter(returned, "row", scatter_dimension=0, tiled=True) / spectral_scale

    first_term = normal_apply(vectors) - vectors
    filtered = 2.0 * (normal_apply(first_term) - first_term) - vectors
    return filtered


def solution(mesh):
    placed = (
        P(("ens", "row", "col"), None),
        P(("ens", "row", "col"), None),
        P(("ens", "row", "col")),
        P(),
        P("ens", None),
    )
    return jax.shard_map(
        local, mesh=mesh, in_specs=placed, out_specs=P(("ens", "row", "col"), None), check_vma=False
    )
```

profile of v0, /device:TPU:0, one launch (start us, length us, event | category | flops | bytes accessed | tf_op | source)
XLA Modules:
  0.0 560.3 jit_solution(4432875654553335063)
XLA Ops:
  6.5 0.0 all-gather.10.cloned.1.call-start
  6.5 1.3 reduce_sum.36
  7.9 1.4 multiply_reduce_fusion
  9.3 2.3 subtract_multiply_fusion
  11.6 0.0 all-gather.10.cloned.1.call-update
  11.6 0.0 all-gather.8.cloned.1.call-start
  11.7 0.7 all-gather.8.cloned.1.call-update
  12.4 0.0 all-gather.12.cloned.1.call-start
  12.4 0.7 all-gather.12.cloned.1.call-update
  13.1 0.0 reduce-scatter.5.cloned.1.call-start
  13.2 0.0 copy-done.2
  13.2 0.0 copy-done.3
  13.2 0.1 select_reduce_fusion
  13.3 6.2 %all-gather = f32[4,1,768]{2,1,0:T(1,128)S(1)} all-gather(f32[1,1,768]{2,1,0:T(1,128)S(1)} %reshape.49), channel_id=1, replica_groups=mesh['ens'=2,'row'=4,'col'=4] {'col'}, dimensions={0}, use_global_device_ids=true | all-gather | bytes 15360 | tf_op jit(solution)/shard_map/all_gather | solution.py:30
  19.5 0.9 fusion.1
  20.5 57.5 %all-gather.10.cloned.1.call-done = f32[3072,256]{1,0:T(8,128)} async-done(((f32[768,256]{1,0:T(8,128)}), f32[3072,256]{1,0:T(8,128)}) %all-gather.10.cloned.1.call-update) | async-done | bytes 3145744 | tf_op jit(solution)/shard_map/all_gather | solution.py:39
  78.0 28.7 %all-gather.8.cloned.1.call-done = f32[3072,256]{1,0:T(8,128)} async-done(((f32[768,256]{1,0:T(8,128)}), f32[3072,256]{1,0:T(8,128)}) %all-gather.8.cloned.1.call-update) | async-done | bytes 3145744 | tf_op jit(solution)/shard_map/all_gather | solution.py:29
  106.7 40.0 %fusion = f32[3072,3072]{1,0:T(8,128)} fusion(f32[3072,256]{1,0:T(8,128)} %all-gather.8.cloned.1.call-done, f32[3072,256]{1,0:T(8,128)} %all-gather.10.cloned.1.call-done, f32[3072]{0:T(1024)S(1)} %bitcast.15, f32[8,3072]{1,0:T(8,128)S(1)} %fusion.1), kind=kOutput, calls=%fused_computation.1 | convolution fusion | flops 29019340800 | bytes 44150784 | tf_op jit(solution)/shard_map/dot_general | solution.py:55
  146.7 34.9 %fusion.21 = f32[3072,128]{1,0:T(8,128)} fusion(f32[3072,3072]{1,0:T(8,128)} %fusion, f32[3072,128]{1,0:T(8,128)} %all-gather.12.cloned.1.call-done), kind=kOutput, calls=%fused_computation.39 | convolution fusion | flops 14495514624 | bytes 40894464 | tf_op jit(solution)/shard_map/dot_general | solution.py:68
  181.6 0.0 reduce-scatter.5.cloned.1.call-update
  181.6 0.0 all-gather.14.cloned.1.call-start
  181.7 28.1 %reduce-scatter.5.cloned.1.call-done = f32[768,128]{1,0:T(8,128)} async-done(((f32[3072,128]{1,0:T(8,128)}), f32[768,128]{1,0:T(8,128)}) %reduce-scatter.5.cloned.1.call-update) | async-done | bytes 393232 | tf_op jit(solution)/shard_map/reduce_scatter | solution.py:86
  209.8 0.0 all-gather.14.cloned.1.call-update
  209.8 0.0 copy-start
  209.8 0.0 reduce-scatter.7.cloned.1.call-start
  209.9 21.0 %all-gather.14.cloned.1.call-done = f32[3072,128]{1,0:T(8,128)} async-done(((f32[768,128]{1,0:T(8,128)}), f32[3072,128]{1,0:T(8,128)}) %all-gather.14.cloned.1.call-update) | async-done | bytes 1572880 | tf_op jit(solution)/shard_map/all_gather | solution.py:87
  230.9 64.5 %fusion.22 = f32[3072,128]{1,0:T(8,128)} fusion(f32[3072,3072]{1,0:T(8,128)} %fusion, f32[3072,128]{1,0:T(8,128)} %all-gather.14.cloned.1.call-done), kind=kOutput, calls=%fused_computation.40 | convolution fusion | flops 14495514624 | bytes 40894464 | tf_op jit(solution)/shard_map/dot_general | solution.py:76
  295.4 0.0 reduce-scatter.7.cloned.1.call-update
  295.4 0.0 all-gather.16.cloned.1.call-start
  295.5 0.6 multiply_reduce_fusion.1
  296.7 34.3 %reduce-scatter.7.cloned.1.call-done = f32[768,128]{1,0:T(8,128)} async-done(((f32[3072,128]{1,0:T(8,128)}), f32[768,128]{1,0:T(8,128)}) %reduce-scatter.7.cloned.1.call-update) | async-done | bytes 393232 | tf_op jit(solution)/shard_map/reduce_scatter | solution.py:88
  331.0 0.0 copy-done
  331.0 1.8 divide_subtract_fusion
  332.8 0.0 all-gather.16.cloned.1.call-update
  332.8 0.0 reduce-scatter.9.cloned.1.call-start
  332.9 36.0 %all-gather.16.cloned.1.call-done = f32[3072,128]{1,0:T(8,128)} async-done(((f32[768,128]{1,0:T(8,128)}), f32[3072,128]{1,0:T(8,128)}) %all-gather.16.cloned.1.call-update) | async-done | bytes 1572880 | tf_op jit(solution)/shard_map/all_gather | solution.py:85
  368.8 34.7 %fusion.23 = f32[3072,128]{1,0:T(8,128)} fusion(f32[3072,3072]{1,0:T(8,128)} %fusion, f32[3072,128]{1,0:T(8,128)} %all-gather.16.cloned.1.call-done), kind=kOutput, calls=%fused_computation.41 | convolution fusion | flops 14495514624 | bytes 40894464 | tf_op jit(solution)/shard_map/dot_general | solution.py:68
  403.6 0.0 reduce-scatter.9.cloned.1.call-update
  403.6 0.0 all-gather.18.cloned.1.call-start
  403.6 27.0 %reduce-scatter.9.cloned.1.call-done = f32[768,128]{1,0:T(8,128)} async-done(((f32[3072,128]{1,0:T(8,128)}), f32[768,128]{1,0:T(8,128)}) %reduce-scatter.9.cloned.1.call-update) | async-done | bytes 393232 | tf_op jit(solution)/shard_map/reduce_scatter | solution.py:86
  430.6 0.0 all-gather.18.cloned.1.call-update
  430.6 0.0 copy-start.1
  430.6 0.0 reduce-scatter.11.cloned.1.call-start
  430.7 21.1 %all-gather.18.cloned.1.call-done = f32[3072,128]{1,0:T(8,128)} async-done(((f32[768,128]{1,0:T(8,128)}), f32[3072,128]{1,0:T(8,128)}) %all-gather.18.cloned.1.call-update) | async-done | bytes 1572880 | tf_op jit(solution)/shard_map/all_gather | solution.py:87
  451.8 64.0 %fusion.24 = f32[3072,128]{1,0:T(8,128)} fusion(f32[3072,3072]{1,0:T(8,128)} %fusion, f32[3072,128]{1,0:T(8,128)} %all-gather.18.cloned.1.call-done), kind=kOutput, calls=%fused_computation.42 | convolution fusion | flops 14495514624 | bytes 40894464 | tf_op jit(solution)/shard_map/dot_general | solution.py:76
  515.8 0.0 reduce-scatter.11.cloned.1.call-update
  515.9 35.6 %reduce-scatter.11.cloned.1.call-done = f32[768,128]{1,0:T(8,128)} async-done(((f32[3072,128]{1,0:T(8,128)}), f32[768,128]{1,0:T(8,128)}) %reduce-scatter.11.cloned.1.call-update) | async-done | bytes 393232 | tf_op jit(solution)/shard_map/reduce_scatter | solution.py:88
  551.5 1.8 multiply_subtract_fusion
  (8 shorter events, 0.0 us)
Async XLA Ops:
  6.5 6.6 %copy-start.2 = (s32[768]{0:T(1024)S(1)}, s32[768]{0:T(1024)}, u32[]{:S(2)}) copy-start(s32[768]{0:T(1024)} %param.7) | copy-start | bytes 9220
  6.5 6.7 %copy-start.3 = (f32[16]{0:T(128)S(1)}, f32[16]{0:T(128)}, u32[]{:S(2)}) copy-start(f32[16]{0:T(128)} %param.8) | copy-start | bytes 196
  6.5 71.4 %all-gather.10.cloned.1.call-start = ((), (), s32[]{:S(2)}) async-start(), calls=%async_computation.5 | async-start | bytes 3932160 | tf_op jit(solution)/shard_map/all_gather | solution.py:39
  11.6 95.1 %all-gather.8.cloned.1.call-start = ((), (), s32[]{:S(2)}) async-start(), calls=%async_computation.4 | async-start | bytes 3932160 | tf_op jit(solution)/shard_map/all_gather | solution.py:29
  12.4 134.3 %all-gather.12.cloned.1.call-start = ((), (), s32[]{:S(2)}) async-start(), calls=%async_computation.6 | async-start | bytes 1966080 | tf_op jit(solution)/shard_map/all_gather | solution.py:85
  13.1 196.7 %reduce-scatter.5.cloned.1.call-start = ((), (), s32[]{:S(2)}) async-start(), calls=%async_computation.7 | async-start | bytes 1966080 | tf_op jit(solution)/shard_map/reduce_scatter | solution.py:86
  181.6 49.3 %all-gather.14.cloned.1.call-start = ((), (), s32[]{:S(2)}) async-start(), calls=%async_computation.8 | async-start | bytes 1966080 | tf_op jit(solution)/shard_map/all_gather | solution.py:87
  209.8 121.2 %copy-start = (f32[768,128]{1,0:T(8,128)S(1)}, f32[768,128]{1,0:T(8,128)}, u32[]{:S(2)}) copy-start(f32[768,128]{1,0:T(8,128)} %param.6) | copy-start | bytes 1179652
  209.8 121.2 %reduce-scatter.7.cloned.1.call-start = ((), (), s32[]{:S(2)}) async-start(), calls=%async_computation.9 | async-start | bytes 1966080 | tf_op jit(solution)/shard_map/reduce_scatter | solution.py:88
  295.4 73.4 %all-gather.16.cloned.1.call-start = ((), (), s32[]{:S(2)}) async-start(), calls=%async_computation.10 | async-start | bytes 1966080 | tf_op jit(solution)/shard_map/all_gather | solution.py:85
  332.8 97.8 %reduce-scatter.9.cloned.1.call-start = ((), (), s32[]{:S(2)}) async-start(), calls=%async_computation.11 | async-start | bytes 1966080 | tf_op jit(solution)/shard_map/reduce_scatter | solution.py:86
  403.6 48.2 %all-gather.18.cloned.1.call-start = ((), (), s32[]{:S(2)}) async-start(), calls=%async_computation.12 | async-start | bytes 1966080 | tf_op jit(solution)/shard_map/all_gather | solution.py:87
  430.6 120.8 %copy-start.1 = (f32[768,128]{1,0:T(8,128)S(1)}, f32[768,128]{1,0:T(8,128)}, u32[]{:S(2)}) copy-start(f32[768,128]{1,0:T(8,128)} %reduce-scatter.7.cloned.1.call-done) | copy-start | bytes 1179652
  430.6 120.8 %reduce-scatter.11.cloned.1.call-start = ((), (), s32[]{:S(2)}) async-start(), calls=%async_computation.13 | async-start | bytes 1966080 | tf_op jit(solution)/shard_map/reduce_scatter | solution.py:88
Sparse Core Ops, SparseCore 0:
  11.8 66.1 all-gather.9
  79.5 27.1 all-gather.7
  108.3 37.0 all-gather.11
  181.7 28.0 reduce-scatter.4
  211.2 19.6 all-gather.13
  295.5 35.4 reduce-scatter.6
  332.9 35.8 all-gather.15
  403.7 26.8 reduce-scatter.8
  432.2 19.6 all-gather.17
  516.0 35.4 reduce-scatter.10
where the time goes:
time: 568 us; the launch traced here: 560 us
  waiting for transfers between devices  291 us (51%)
  matrix products  239 us (42%)
  between operations  14.5 us (3%)
  other arithmetic  9.36 us (2%)
  blocking collectives  6.21 us (1%)
    dot_general x2, matrix products, backward_add(): lax.dot_general(affinity, shard_piece, (((0,), (0,)), ((), ())), precisio...  129 us
    reduce_scatter x2, waiting for transfers between devices, normal_apply(): lax.psum_scatter(returned, 'row', scatter_dimension=0, tiled=True)  69.9 us
    dot_general x2, matrix products, forward_add(): jnp.dot(affinity, shard_piece, precision=lax.Precision.HIGHEST, preferred...  69.6 us
    all_gather x1, waiting for transfers between devices, local(): shard_piece = lax.all_gather(z_own, 'row', axis=0, tiled=True)  57.5 us
    reduce_scatter x2, waiting for transfers between devices, normal_apply(): product = lax.psum_scatter(product, 'col', scatter_dimension=0, tiled=True)  55.1 us
    all_gather x2, waiting for transfers between devices, normal_apply(): returned = backward_add(lax.all_gather(product, 'col', axis=0, tiled=True))  42.1 us
    dot_general x1, matrix products, local(): lax.dot_general(z_rows, shard_piece, (((1,), (1,)), ((), ())), precision=...  40 us
    all_gather x2, waiting for transfers between devices, normal_apply(): product = forward_add(lax.all_gather(field_in, 'row', axis=0, tiled=True))  36 us
  transfers between devices with their start and end apart: 10, of which 9 were waited for; matrix products, arithmetic and copies ran while one was open for 7% of the time, Pallas kernels for 0%

commit v1 on v0

--- a/solution.py
+++ b/solution.py
@@ -5,6 +5,24 @@
 
 N = 12288
 sharpness = 12.0
+
+
+def gather_around(shard, axis, dim):
+    ways, here, step = (lax.axis_size(axis), lax.axis_index(axis), shard.shape[dim])
+    shape = [n * ways if d == dim else n for d, n in enumerate(shard.shape)]
+    full = lax.dynamic_update_slice_in_dim(
+        jnp.zeros(shape, shard.dtype), shard, here * step, axis=dim
+    )
+    going_up = going_down = shard
+    for far in range(1, ways // 2 + 1):
+        going_up = lax.ppermute(going_up, axis, [(d, (d + 1) % ways) for d in range(ways)])
+        full = lax.dynamic_update_slice_in_dim(full, going_up, (here - far) % ways * step, axis=dim)
+        if 2 * far < ways:
+            going_down = lax.ppermute(going_down, axis, [(d, (d - 1) % ways) for d in range(ways)])
+            full = lax.dynamic_update_slice_in_dim(
+                full, going_down, (here + far) % ways * step, axis=dim
+            )
+    return full
 
 
 def standardize(series):
@@ -84,7 +102,7 @@
     def normal_apply(field_in):
         product = forward_add(lax.all_gather(field_in, "row", axis=0, tiled=True))
         product = lax.psum_scatter(product, "col", scatter_dimension=0, tiled=True)
-        returned = backward_add(lax.all_gather(product, "col", axis=0, tiled=True))
+        returned = backward_add(gather_around(product, "col", 0))
         return lax.psum_scatter(returned, "row", scatter_dimension=0, tiled=True) / spectral_scale
 
     first_term = normal_apply(vectors) - vectors

time: 568 us -> 560 us (0.986)
  waiting for transfers between devices: 291 us -> 281 us
    all_gather x2 -> x0, waiting for transfers between devices: 42.1 us -> none  [normal_apply(): returned = backward_add(lax.all_gather(product, 'col', axis=0, tiled=True))]
    ppermute x0 -> x6, waiting for transfers between devices: none -> 32.4 us  [the longest x4 32.4 us: gather_around(): lax.ppermute(going_up, axis, [(d, (d + 1) % ways) for d in range(ways)])]
    all_gather x1, waiting for transfers between devices: 57.5 us -> 65 us  [local(): shard_piece = lax.all_gather(z_own, 'row', axis=0, tiled=True)]
    all_gather x1, waiting for transfers between devices: 28.7 us -> 22.5 us  [local(): lax.all_gather(z_own, 'col', axis=0, tiled=True)]
  transfers between devices with their start and end apart: 10 -> 14, of which waited for: 9 -> 11; matrix products, arithmetic and copies ran while one was open for 7% -> 8% of each run, Pallas kernels for 0% -> 0%
where the time goes in v1:
time: 560 us; the launch traced here: 553 us
  waiting for transfers between devices  281 us (50%)
  matrix products  239 us (43%)
  between operations  14.6 us (3%)
  other arithmetic  8.3 us (1%)
  blocking collectives  6.21 us (1%)
    dot_general x2, matrix products, backward_add(): lax.dot_general(affinity, shard_piece, (((0,), (0,)), ((), ())), precisio...  128 us
    dot_general x2, matrix products, forward_add(): jnp.dot(affinity, shard_piece, precision=lax.Precision.HIGHEST, preferred...  69.6 us
    reduce_scatter x2, waiting for transfers between devices, normal_apply(): lax.psum_scatter(returned, 'row', scatter_dimension=0, tiled=True)  69.5 us
    all_gather x1, waiting for transfers between devices, local(): shard_piece = lax.all_gather(z_own, 'row', axis=0, tiled=True)  65 us
    reduce_scatter x2, waiting for transfers between devices, normal_apply(): product = lax.psum_scatter(product, 'col', scatter_dimension=0, tiled=True)  53.7 us
    dot_general x1, matrix products, local(): lax.dot_general(z_rows, shard_piece, (((1,), (1,)), ((), ())), precision=...  40.2 us
    all_gather x2, waiting for transfers between devices, normal_apply(): product = forward_add(lax.all_gather(field_in, 'row', axis=0, tiled=True))  36 us
    ppermute x4, waiting for transfers between devices, gather_around(): lax.ppermute(going_up, axis, [(d, (d + 1) % ways) for d in range(ways)])  32.4 us
  transfers between devices with their start and end apart: 14, of which 11 were waited for; matrix products, arithmetic and copies ran while one was open for 8% of the time, Pallas kernels for 0%

profile of v1, /device:TPU:0, one launch (start us, length us, event | category | flops | bytes accessed | tf_op | source)
XLA Modules:
  0.0 552.7 jit_solution(3224318714162124331)
XLA Ops:
  6.5 1.4 reduce_sum.36
  7.9 1.4 multiply_reduce_fusion
  9.4 0.0 copy-start.5
  9.4 0.0 copy-start.6
  9.4 1.2 subtract_multiply_fusion
  10.6 0.0 all-gather.6.cloned.1.call-update
  10.6 0.0 all-gather.8.cloned.1.call-start
  10.7 0.7 all-gather.8.cloned.1.call-update
  11.4 0.0 all-gather.10.cloned.1.call-start
  11.4 0.7 all-gather.10.cloned.1.call-update
  12.1 0.0 reduce-scatter.5.cloned.1.call-start
  12.2 0.1 select_reduce_fusion
  12.3 6.2 %all-gather = f32[4,1,768]{2,1,0:T(1,128)S(1)} all-gather(f32[1,1,768]{2,1,0:T(1,128)S(1)} %reshape.49), channel_id=1, replica_groups=mesh['ens'=2,'row'=4,'col'=4] {'col'}, dimensions={0}, use_global_device_ids=true | all-gather | bytes 15360 | tf_op jit(solution)/shard_map/all_gather | solution.py:48
  18.5 0.9 fusion.1
  19.4 22.5 %all-gather.6.cloned.1.call-done = f32[3072,256]{1,0:T(8,128)} async-done(((f32[768,256]{1,0:T(8,128)}), f32[3072,256]{1,0:T(8,128)}) %all-gather.6.cloned.1.call-update) | async-done | bytes 3145744 | tf_op jit(solution)/shard_map/all_gather | solution.py:47
  42.0 65.0 %all-gather.8.cloned.1.call-done = f32[3072,256]{1,0:T(8,128)} async-done(((f32[768,256]{1,0:T(8,128)}), f32[3072,256]{1,0:T(8,128)}) %all-gather.8.cloned.1.call-update) | async-done | bytes 3145744 | tf_op jit(solution)/shard_map/all_gather | solution.py:57
  107.0 40.2 %fusion = f32[3072,3072]{1,0:T(8,128)} fusion(f32[3072,256]{1,0:T(8,128)} %all-gather.6.cloned.1.call-done, f32[3072,256]{1,0:T(8,128)} %all-gather.8.cloned.1.call-done, f32[3072]{0:T(1024)S(1)} %bitcast.15, f32[8,3072]{1,0:T(8,128)S(1)} %fusion.1), kind=kOutput, calls=%fused_computation.1 | convolution fusion | flops 29019340800 | bytes 44150784 | tf_op jit(solution)/shard_map/dot_general | solution.py:73
  147.2 34.9 %fusion.21 = f32[3072,128]{1,0:T(8,128)} fusion(f32[3072,3072]{1,0:T(8,128)} %fusion, f32[3072,128]{1,0:T(8,128)} %all-gather.10.cloned.1.call-done), kind=kOutput, calls=%fused_computation.47 | convolution fusion | flops 14495514624 | bytes 40894464 | tf_op jit(solution)/shard_map/dot_general | solution.py:86
  182.1 0.0 reduce-scatter.5.cloned.1.call-update
  182.1 0.0 reduce-scatter.7.cloned.1.call-start
  182.2 26.8 %reduce-scatter.5.cloned.1.call-done = f32[768,128]{1,0:T(8,128)} async-done(((f32[3072,128]{1,0:T(8,128)}), f32[768,128]{1,0:T(8,128)}) %reduce-scatter.5.cloned.1.call-update) | async-done | bytes 393232 | tf_op jit(solution)/shard_map/reduce_scatter | solution.py:104
  208.9 0.0 collective-permute-start
  208.9 1.7 collective-permute-start.1
  210.7 9.2 %collective-permute-done = f32[768,128]{1,0:T(8,128)S(1)} collective-permute-done((f32[768,128]{1,0:T(8,128)}, f32[768,128]{1,0:T(8,128)S(1)}, u32[]{:S(2)}, u32[]{:S(2)}) %collective-permute-start) | collective-permute-done | bytes 393248 | tf_op jit(solution)/shard_map/ppermute | solution.py:18
  219.9 0.1 broadcast.106.clone
  220.2 6.9 %collective-permute-done.2 = f32[768,128]{1,0:T(8,128)S(1)} collective-permute-done((f32[768,128]{1,0:T(8,128)S(1)}, f32[768,128]{1,0:T(8,128)S(1)}, u32[]{:S(2)}, u32[]{:S(2)}) %collective-permute-start.2) | collective-permute-done | bytes 393248 | tf_op jit(solution)/shard_map/ppermute | solution.py:18
  227.2 64.3 %fusion.22 = f32[3072,128]{1,0:T(8,128)} fusion(f32[3072,3072]{1,0:T(8,128)} %fusion, f32[3072,128]{1,0:T(8,128)S(1)} %constant_dynamic-update-slice_fusion.4), kind=kOutput, calls=%fused_computation.48 | convolution fusion | flops 14495514624 | bytes 40894464 | tf_op jit(solution)/shard_map/dot_general | solution.py:94
  291.4 0.0 copy-start.1
  291.5 0.0 reduce-scatter.7.cloned.1.call-update
  291.5 0.0 all-gather.12.cloned.1.call-start
  291.5 0.6 multiply_reduce_fusion.1
  292.8 34.1 %reduce-scatter.7.cloned.1.call-done = f32[768,128]{1,0:T(8,128)} async-done(((f32[3072,128]{1,0:T(8,128)}), f32[768,128]{1,0:T(8,128)}) %reduce-scatter.7.cloned.1.call-update) | async-done | bytes 393232 | tf_op jit(solution)/shard_map/reduce_scatter | solution.py:106
  326.8 1.8 divide_subtract_fusion
  328.6 0.0 all-gather.12.cloned.1.call-update
  328.7 0.0 reduce-scatter.9.cloned.1.call-start
  328.7 36.0 %all-gather.12.cloned.1.call-done = f32[3072,128]{1,0:T(8,128)} async-done(((f32[768,128]{1,0:T(8,128)}), f32[3072,128]{1,0:T(8,128)}) %all-gather.12.cloned.1.call-update) | async-done | bytes 1572880 | tf_op jit(solution)/shard_map/all_gather | solution.py:103
  364.7 34.7 %fusion.23 = f32[3072,128]{1,0:T(8,128)} fusion(f32[3072,3072]{1,0:T(8,128)} %fusion, f32[3072,128]{1,0:T(8,128)} %all-gather.12.cloned.1.call-done), kind=kOutput, calls=%fused_computation.49 | convolution fusion | flops 14495514624 | bytes 40894464 | tf_op jit(solution)/shard_map/dot_general | solution.py:86
  399.4 0.0 reduce-scatter.9.cloned.1.call-update
  399.4 0.0 reduce-scatter.11.cloned.1.call-start
  399.4 27.0 %reduce-scatter.9.cloned.1.call-done = f32[768,128]{1,0:T(8,128)} async-done(((f32[3072,128]{1,0:T(8,128)}), f32[768,128]{1,0:T(8,128)}) %reduce-scatter.9.cloned.1.call-update) | async-done | bytes 393232 | tf_op jit(solution)/shard_map/reduce_scatter | solution.py:104
  426.4 1.7 collective-permute-start.4
  428.2 9.2 %collective-permute-done.3 = f32[768,128]{1,0:T(8,128)S(1)} collective-permute-done((f32[768,128]{1,0:T(8,128)}, f32[768,128]{1,0:T(8,128)S(1)}, u32[]{:S(2)}, u32[]{:S(2)}) %collective-permute-start.3) | collective-permute-done | bytes 393248 | tf_op jit(solution)/shard_map/ppermute | solution.py:18
  437.4 0.1 broadcast.106
  437.6 6.9 %collective-permute-done.5 = f32[768,128]{1,0:T(8,128)S(1)} collective-permute-done((f32[768,128]{1,0:T(8,128)S(1)}, f32[768,128]{1,0:T(8,128)S(1)}, u32[]{:S(2)}, u32[]{:S(2)}) %collective-permute-start.5) | collective-permute-done | bytes 393248 | tf_op jit(solution)/shard_map/ppermute | solution.py:18
  444.6 63.8 %fusion.24 = f32[3072,128]{1,0:T(8,128)} fusion(f32[3072,3072]{1,0:T(8,128)} %fusion, f32[3072,128]{1,0:T(8,128)S(1)} %constant_dynamic-update-slice_fusion), kind=kOutput, calls=%fused_computation.50 | convolution fusion | flops 14495514624 | bytes 40894464 | tf_op jit(solution)/shard_map/dot_general | solution.py:94
  508.4 0.0 reduce-scatter.11.cloned.1.call-update
  508.4 35.4 %reduce-scatter.11.cloned.1.call-done = f32[768,128]{1,0:T(8,128)} async-done(((f32[3072,128]{1,0:T(8,128)}), f32[768,128]{1,0:T(8,128)}) %reduce-scatter.11.cloned.1.call-update) | async-done | bytes 393232 | tf_op jit(solution)/shard_map/reduce_scatter | solution.py:106
  543.8 1.8 multiply_subtract_fusion
  (30 shorter events, 0.3 us)
Async XLA Ops:
  6.5 2.8 copy-start
  6.5 35.5 %all-gather.6.cloned.1.call-start = ((), (), s32[]{:S(2)}) async-start(), calls=%async_computation.4 | async-start | bytes 3932160 | tf_op jit(solution)/shard_map/all_gather | solution.py:47
  9.4 2.8 copy-start.5
  9.4 2.8 copy-start.6
  10.6 96.4 %all-gather.8.cloned.1.call-start = ((), (), s32[]{:S(2)}) async-start(), calls=%async_computation.5 | async-start | bytes 3932160 | tf_op jit(solution)/shard_map/all_gather | solution.py:57
  11.4 135.9 %all-gather.10.cloned.1.call-start = ((), (), s32[]{:S(2)}) async-start(), calls=%async_computation.6 | async-start | bytes 1966080 | tf_op jit(solution)/shard_map/all_gather | solution.py:103
  12.1 196.8 %reduce-scatter.5.cloned.1.call-start = ((), (), s32[]{:S(2)}) async-start(), calls=%async_computation.7 | async-start | bytes 1966080 | tf_op jit(solution)/shard_map/reduce_scatter | solution.py:104
  182.1 144.7 %reduce-scatter.7.cloned.1.call-start = ((), (), s32[]{:S(2)}) async-start(), calls=%async_computation.8 | async-start | bytes 1966080 | tf_op jit(solution)/shard_map/reduce_scatter | solution.py:106
  208.9 11.1 %copy-start.3 = (f32[768,128]{1,0:T(8,128)S(1)}, f32[768,128]{1,0:T(8,128)}, u32[]{:S(2)}) copy-start(f32[768,128]{1,0:T(8,128)} %reduce-scatter.5.cloned.1.call-done) | copy-start | bytes 1179652
  208.9 11.0 %collective-permute-start = (f32[768,128]{1,0:T(8,128)}, f32[768,128]{1,0:T(8,128)S(1)}, u32[]{:S(2)}, u32[]{:S(2)}) collective-permute-start(f32[768,128]{1,0:T(8,128)} %reduce-scatter.5.cloned.1.call-done), channel_id=1, source_target_pairs={{0,1},{1,2},{2,3},{3,0},{4,5},{5,6},{6,7},{7,4},{8,9},{9,10},{10,1... | collective-permute-start | bytes 1179656 | tf_op jit(solution)/shard_map/ppermute | solution.py:18
  208.9 11.2 %collective-permute-start.1 = (f32[768,128]{1,0:T(8,128)}, f32[768,128]{1,0:T(8,128)S(1)}, u32[]{:S(2)}, u32[]{:S(2)}) collective-permute-start(f32[768,128]{1,0:T(8,128)} %reduce-scatter.5.cloned.1.call-done), channel_id=1, source_target_pairs={{0,3},{1,0},{2,1},{3,2},{4,7},{5,4},{6,5},{7,6},{8,11},{9,8},{10,9... | collective-permute-start | bytes 1179656 | tf_op jit(solution)/shard_map/ppermute | solution.py:21
  219.9 7.2 %collective-permute-start.2 = (f32[768,128]{1,0:T(8,128)S(1)}, f32[768,128]{1,0:T(8,128)S(1)}, u32[]{:S(2)}, u32[]{:S(2)}) collective-permute-start(f32[768,128]{1,0:T(8,128)S(1)} %collective-permute-done), channel_id=1, source_target_pairs={{0,1},{1,2},{2,3},{3,0},{4,5},{5,6},{6,7},{7,4},{8,9},{9,10},{10,1... | collective-permute-start | bytes 1179656 | tf_op jit(solution)/shard_map/ppermute | solution.py:18
  291.4 35.4 %copy-start.1 = (f32[768,128]{1,0:T(8,128)S(1)}, f32[768,128]{1,0:T(8,128)}, u32[]{:S(2)}) copy-start(f32[768,128]{1,0:T(8,128)} %param.6) | copy-start | bytes 1179652
  291.5 73.2 %all-gather.12.cloned.1.call-start = ((), (), s32[]{:S(2)}) async-start(), calls=%async_computation.9 | async-start | bytes 1966080 | tf_op jit(solution)/shard_map/all_gather | solution.py:103
  328.7 97.8 %reduce-scatter.9.cloned.1.call-start = ((), (), s32[]{:S(2)}) async-start(), calls=%async_computation.10 | async-start | bytes 1966080 | tf_op jit(solution)/shard_map/reduce_scatter | solution.py:104
  399.4 144.4 %reduce-scatter.11.cloned.1.call-start = ((), (), s32[]{:S(2)}) async-start(), calls=%async_computation.11 | async-start | bytes 1966080 | tf_op jit(solution)/shard_map/reduce_scatter | solution.py:106
  426.4 11.1 %copy-start.4 = (f32[768,128]{1,0:T(8,128)S(1)}, f32[768,128]{1,0:T(8,128)}, u32[]{:S(2)}) copy-start(f32[768,128]{1,0:T(8,128)} %reduce-scatter.9.cloned.1.call-done) | copy-start | bytes 1179652
  426.4 11.0 %collective-permute-start.3 = (f32[768,128]{1,0:T(8,128)}, f32[768,128]{1,0:T(8,128)S(1)}, u32[]{:S(2)}, u32[]{:S(2)}) collective-permute-start(f32[768,128]{1,0:T(8,128)} %reduce-scatter.9.cloned.1.call-done), channel_id=1, source_target_pairs={{0,1},{1,2},{2,3},{3,0},{4,5},{5,6},{6,7},{7,4},{8,9},{9,10},{10,1... | collective-permute-start | bytes 1179656 | tf_op jit(solution)/shard_map/ppermute | solution.py:18
  426.4 11.2 %collective-permute-start.4 = (f32[768,128]{1,0:T(8,128)}, f32[768,128]{1,0:T(8,128)S(1)}, u32[]{:S(2)}, u32[]{:S(2)}) collective-permute-start(f32[768,128]{1,0:T(8,128)} %reduce-scatter.9.cloned.1.call-done), channel_id=1, source_target_pairs={{0,3},{1,0},{2,1},{3,2},{4,7},{5,4},{6,5},{7,6},{8,11},{9,8},{10,9... | collective-permute-start | bytes 1179656 | tf_op jit(solution)/shard_map/ppermute | solution.py:21
  437.4 7.2 %collective-permute-start.5 = (f32[768,128]{1,0:T(8,128)S(1)}, f32[768,128]{1,0:T(8,128)S(1)}, u32[]{:S(2)}, u32[]{:S(2)}) collective-permute-start(f32[768,128]{1,0:T(8,128)S(1)} %collective-permute-done.3), channel_id=1, source_target_pairs={{0,1},{1,2},{2,3},{3,0},{4,5},{5,6},{6,7},{7,4},{8,9},{9,10},{10,1... | collective-permute-start | bytes 1179656 | tf_op jit(solution)/shard_map/ppermute | solution.py:18
  508.4 35.4 %copy-start.2 = (f32[768,128]{1,0:T(8,128)S(1)}, f32[768,128]{1,0:T(8,128)}, u32[]{:S(2)}) copy-start(f32[768,128]{1,0:T(8,128)} %reduce-scatter.7.cloned.1.call-done) | copy-start | bytes 1179652
Sparse Core Ops, SparseCore 0:
  10.7 31.2 all-gather.5
  43.6 63.4 all-gather.7
  108.6 35.6 all-gather.9
  182.2 26.6 reduce-scatter.4
  291.6 35.1 reduce-scatter.6
  328.8 35.8 all-gather.11
  399.5 26.8 reduce-scatter.8
  508.5 35.2 reduce-scatter.10
